TPU v7x, 32 devices: a whole 2x2x4 slice. The times are simulated.
32 devices in a mesh: gx: 4 (over z), gy: 2 (over y), gz: 4 (over x, core).
Axes of the slice: x: 2, y: 2, z: 4, core: 2. Of those that a mesh axis runs over, the one named last changes fastest.
Arguments:
- positions: float32 [3, 131072], P(None, ('gx', 'gy', 'gz'))
- velocities: float32 [3, 131072], P(None, ('gx', 'gy', 'gz')), may hold values from -6 to 6
- forces_old: float32 [3, 131072], P(None, ('gx', 'gy', 'gz')), may hold values from -6 to 6
- inv_mass: float32 [131072], P(('gx', 'gy', 'gz')), may hold values from 0.25 to 4
- charges: float32 [131072], P(('gx', 'gy', 'gz')), may hold values from -3 to 3
- block_species: int32 [1024], P(('gx', 'gy', 'gz')), may hold values from 0 to 3
- sigma_table: float32 [4], replicated, may hold values from 0.25 to 0.5
- epsilon_table: float32 [4], replicated, may hold values from 0.02 to 0.2
- tower_index: int32 [32, 64], P(('gx', 'gy', 'gz')), may hold values from 0 to 127
- plate_index: int32 [32, 64], P(('gx', 'gy', 'gz')), may hold values from 0 to 287
- tile_counts: int32 [32], P(('gx', 'gy', 'gz')), may hold values from 1 to 64, as said below
- exclusions: int32 [32, 64, 16, 128], P(('gx', 'gy', 'gz')), may hold values from 0 to 255, as said below
- mig_block: int32 [32, 4], P(('gx', 'gy', 'gz')), may hold values from 0 to 31, as said below
- mig_dest: int32 [32, 4], P(('gx', 'gy', 'gz')), may hold values from 0 to 8, as said below
Outputs:
- positions_new: float32 [3, 131072], P(None, ('gx', 'gy', 'gz'))
- velocities_new: float32 [3, 131072], P(None, ('gx', 'gy', 'gz'))
- forces_new: float32 [3, 131072], P(None, ('gx', 'gy', 'gz'))
- arrivals: float32 [6, 32, 8, 512], P(None, ('gx', 'gy', 'gz'))
Inputs may be any that keep to these rules, and one draw needn't show every extreme that they name: `tile_counts`: at most 64 for every box, and exactly 64 for some box; slots at or after a box's count carry no weight. `exclusions`: each of the low eight bits marks one excluded atom pair. `mig_block`: the 4 entries of one box are distinct. `mig_dest`: never 4.
All inputs are finite; a program needn't handle non-finite values.
Results may differ from a plain program's by a relative error of at most 0.0003.
Values sent between devices are 32-bit elements; how exact they have to be, the bound alone decides.
A program may use at most 64 MiB of HBM per device.

v0:
```python
import jax
import jax.numpy as jnp
from jax import lax
from jax.sharding import PartitionSpec as P

time_step = 0.2
soft_core = 0.09
cutoff_sq = 1.44
coulomb_k = 0.5
source_cells = ((0, 0), (0, 2), (0, 4), (2, 0), (2, 4), (4, 0), (4, 2), (4, 4))


def with_halo(value, sides, width):
    for axis, dim in sides:
        count, length = (lax.axis_size(axis), value.shape[dim])
        up = [(i, (i + 1) % count) for i in range(count)]
        down = [(j, i) for i, j in up]
        last = lax.slice_in_dim(value, length - width, length, axis=dim)
        first = lax.slice_in_dim(value, 0, width, axis=dim)
        before = lax.ppermute(last, axis, up)
        after = lax.ppermute(first, axis, down)
        value = jnp.concatenate([before, value, after], axis=dim)
    return value


def tile_terms(tower_rows, plate_rows, mask_words, length_x, length_y):
    tile_width = tower_rows.shape[1]
    raw = tower_rows[0:3, :, None] - plate_rows[0:3, None, :]
    image_x = raw[0] - length_x * jnp.floor(raw[0] / length_x + 0.5)
    image_y = raw[1] - length_y * jnp.floor(raw[1] / length_y + 0.5)
    offsets = jnp.stack([image_x, image_y, raw[2]], axis=0)
    distance_sq = jnp.sum(offsets * offsets, axis=0)
    inverse = 1.0 / (distance_sq + soft_core)
    sigma_pair = 0.5 * (tower_rows[4][:, None] + plate_rows[4][None, :])
    ratio_pair = sigma_pair * sigma_pair * inverse
    ratio_cube = ratio_pair * ratio_pair * ratio_pair
    depth_pair = tower_rows[5][:, None] * plate_rows[5][None, :]
    charge_term = coulomb_k * tower_rows[3][:, None] * plate_rows[3][None, :] * jnp.sqrt(inverse)
    falloff = 1.0 - distance_sq / cutoff_sq
    switch = jnp.where(distance_sq < cutoff_sq, falloff * falloff, 0.0)
    spread = jnp.repeat(mask_words.T, 8, axis=1)
    shifts = jnp.arange(tile_width, dtype=jnp.int32) % 8
    excluded = jnp.bitwise_and(jnp.right_shift(spread, shifts[None, :]), 1)
    kept_pairs = (1 - excluded).astype(jnp.float32)
    strength = (
        (depth_pair * (12.0 * ratio_cube * ratio_cube - 6.0 * ratio_cube) + charge_term)
        * inverse
        * switch
        * kept_pairs
    )
    weighted = strength[None] * offsets
    return (jnp.sum(weighted, axis=2), -jnp.sum(weighted, axis=1))


def local(
    positions,
    velocities,
    forces_old,
    inv_mass,
    charges,
    block_species,
    sigma_table,
    epsilon_table,
    tower_index,
    plate_index,
    tile_counts,
    exclusions,
    mig_block,
    mig_dest,
):
    atom_count = positions.shape[1]
    block_count = block_species.shape[0]
    tile_width = atom_count // block_count
    layers = lax.axis_size("gz")
    length_x = float(lax.axis_size("gx"))
    length_y = float(lax.axis_size("gy"))
    half_kick = velocities + 0.5 * time_step * forces_old * inv_mass[None, :]
    moved = positions + time_step * half_kick
    species_hot = (
        block_species[None, :] == jnp.arange(sigma_table.shape[0], dtype=jnp.int32)[:, None]
    ).astype(jnp.float32)
    tables = jnp.stack([sigma_table, jnp.sqrt(epsilon_table)], axis=0)
    per_block = jnp.dot(tables, species_hot, precision=lax.Precision.HIGHEST)
    per_atom = jnp.repeat(per_block, tile_width, axis=1)
    features = jnp.concatenate([moved, charges[None, :], per_atom], axis=0)
    towers = lax.all_gather(features, "gz", axis=1, tiled=True).reshape(
        6, layers * block_count, tile_width
    )
    own_cell = features.reshape(6, 1, 1, atom_count)
    plate_grid = with_halo(own_cell, (("gx", 1), ("gy", 2)), 1)
    plates = plate_grid.reshape(6, 9 * block_count, tile_width)
    tower_list = tower_index[0]
    plate_list = plate_index[0]
    pair_count = tile_counts[0]
    mask_list = exclusions[0]
    slot_count = tower_list.shape[0]
    group_size = min(16, slot_count)

    def pair_terms(tower_rows, plate_rows, mask_words):
        return tile_terms(tower_rows, plate_rows, mask_words, length_x, length_y)

    def evaluate(group_index, totals):
        on_towers, on_plates = totals
        first_slot = group_index * group_size
        tower_ids = lax.dynamic_slice_in_dim(tower_list, first_slot, group_size)
        plate_ids = lax.dynamic_slice_in_dim(plate_list, first_slot, group_size)
        mask_words = lax.dynamic_slice_in_dim(mask_list, first_slot, group_size, 0)
        tower_tiles = jnp.take(towers, tower_ids, axis=1)
        plate_tiles = jnp.take(plates, plate_ids, axis=1)
        on_tower, on_plate = jax.vmap(pair_terms, in_axes=(1, 1, 0), out_axes=1)(
            tower_tiles, plate_tiles, mask_words
        )
        listed = (first_slot + jnp.arange(group_size, dtype=jnp.int32) < pair_count).astype(
            jnp.float32
        )[None, :, None]
        on_towers = on_towers.at[:, tower_ids].add(on_tower * listed)
        on_plates = on_plates.at[:, plate_ids].add(on_plate * listed)
        return (on_towers, on_plates)

    start = (
        jnp.zeros((3, layers * block_count, tile_width), jnp.float32),
        jnp.zeros((3, 9 * block_count, tile_width), jnp.float32),
    )
    rounds = (pair_count + group_size - 1) // group_size
    on_towers, on_plates = lax.fori_loop(0, rounds, evaluate, start)
    tower_back = lax.psum_scatter(
        on_towers.reshape(3, layers * atom_count), "gz", scatter_dimension=1, tiled=True
    )
    plate_cells = on_plates.reshape(3, 3, 3, atom_count)
    returned = with_halo(plate_cells, (("gx", 1), ("gy", 2)), 1)
    plate_back = jnp.sum(returned[:, 0::2, 0::2], axis=(1, 2))
    forces_new = tower_back + plate_back
    velocity_full = half_kick + 0.5 * time_step * forces_new * inv_mass[None, :]
    leaving = mig_block[0]
    heading = mig_dest[0]
    block_slots = jnp.arange(block_count, dtype=jnp.int32)
    departed = jnp.sum((leaving[:, None] == block_slots[None, :]).astype(jnp.float32), axis=0)
    staying = jnp.repeat(1.0 - departed, tile_width)[None, :]
    positions_new = moved * staying
    velocities_new = velocity_full * staying
    state = jnp.concatenate([moved, velocity_full], axis=0).reshape(6, block_count, tile_width)
    chosen = jnp.take(state, leaving, axis=1)
    targets = (heading[None, :] == jnp.arange(9, dtype=jnp.int32)[:, None]).astype(jnp.float32)
    outgoing = (chosen[:, None] * targets[None, :, :, None]).reshape(
        6, 3, 3, leaving.shape[0] * tile_width
    )
    landed = with_halo(outgoing, (("gx", 1), ("gy", 2)), 1)
    arrivals = jnp.stack(
        [landed[:, row_cell, col_cell] for row_cell, col_cell in source_cells], axis=1
    )[:, None]
    return (positions_new, velocities_new, forces_new, arrivals)


def solution(mesh):
    in_specs = (
        P(None, ("gx", "gy", "gz")),
        P(None, ("gx", "gy", "gz")),
        P(None, ("gx", "gy", "gz")),
        P(("gx", "gy", "gz")),
        P(("gx", "gy", "gz")),
        P(("gx", "gy", "gz")),
        P(),
        P(),
        P(("gx", "gy", "gz"), None),
        P(("gx", "gy", "gz"), None),
        P(("gx", "gy", "gz")),
        P(("gx", "gy", "gz"), None, None, None),
        P(("gx", "gy", "gz"), None),
        P(("gx", "gy", "gz"), None),
    )
    out_specs = (
        P(None, ("gx", "gy", "gz")),
        P(None, ("gx", "gy", "gz")),
        P(None, ("gx", "gy", "gz")),
        P(None, ("gx", "gy", "gz"), None, None),
    )
    return jax.shard_map(local, mesh=mesh, in_specs=in_specs, out_specs=out_specs, check_vma=False)
```

profile of v0, /device:TPU:0, one launch (start us, length us, event | category | flops | bytes accessed | tf_op | source)
XLA Modules:
  0.0 232.1 jit_solution(4710218359998347829)
XLA Ops:
  10.4 1.6 broadcast_multiply_fusion.2
  12.7 3.1 %collective-permute-start = (f32[6,1,1,4096]{3,0,2,1:T(8,128)S(1)}, f32[6,1,1,4096]{3,0,2,1:T(8,128)S(1)}, u32[]{:S(2)}, u32[]{:S(2)}) collective-permute-start(f32[6,1,1,4096]{3,0,2,1:T(8,128)S(1)} %get-tuple-element.216), channel_id=1, source_target_pairs={{0,8},{8,16},{16,24},{24,0},{1,9},{9,17},{17,25},{25,1},{2,10},{10... | collective-permute-start | bytes 294920 | tf_op jit(solution)/shard_map/ppermute | solution.py:20
  15.8 2.1 collective-permute-start.1
  17.9 1.2 fusion.12
  19.1 3.1 %collective-permute-done = f32[6,1,1,4096]{3,0,2,1:T(8,128)S(1)} collective-permute-done((f32[6,1,1,4096]{3,0,2,1:T(8,128)S(1)}, f32[6,1,1,4096]{3,0,2,1:T(8,128)S(1)}, u32[]{:S(2)}, u32[]{:S(2)}) %collective-permute-start) | collective-permute-done | bytes 98336 | tf_op jit(solution)/shard_map/ppermute | solution.py:20
  22.2 1.4 collective-permute-done.1
  23.6 1.6 collective-permute-start.2
  25.7 7.6 %all_gather.3 = f32[6,16384]{1,0:T(8,128)} all-gather(f32[6,4096]{1,0:T(8,128)S(1)} %get-tuple-element.217), channel_id=1, replica_groups=mesh['gx'=4,'gy'=2,'gz'=4] {'gz'}, dimensions={1}, use_global_device_ids=true | all-gather | bytes 491520 | tf_op jit(solution)/shard_map/all_gather | solution.py:86
  35.7 6.9 %collective-permute-done.3 = f32[6,3,1,4096]{3,0,2,1:T(8,128)S(1)} collective-permute-done((f32[6,3,1,4096]{3,0,2,1:T(8,128)S(1)}, f32[6,3,1,4096]{3,0,2,1:T(8,128)S(1)}, u32[]{:S(2)}, u32[]{:S(2)}) %collective-permute-start.3) | collective-permute-done | bytes 294944 | tf_op jit(solution)/shard_map/ppermute | solution.py:21
  42.6 1.2 pad_maximum_fusion.2
  44.7 18.6 %while.14 = (s32[]{:T(128)}, f32[3,128,128]{2,0,1:T(4,128)S(1)}, f32[3,288,128]{2,0,1:T(4,128)}, s32[]{:T(128)}, s32[64]{0:T(128)S(1)}, /*index=5*/f32[6,128,128...) while((s32[]{:T(128)}, f32[3,128,128]{2,0,1:T(4,128)S(1)}, ...), condition=%wide.region_7.8_spmd, body=%wide.region_1.7_spmd.sunk | while | flops 17873908 | bytes 25701420 | solution.py:125
  45.5 1.8 gather_fusion
  47.5 1.6 gather_fusion.1
  50.7 1.3 multiply_reduce_fusion.5
  54.0 2.5 %copy.63 = s32[16,128,128]{2,1,0:T(8,128)} copy(s32[16,128,128]{1,2,0:T(8,128)} %broadcast_bitcast_fusion.5) | data formatting | bytes 2097152 | tf_op jit(solution)/shard_map/while/body/vmap()/reshape | solution.py:41
  56.6 2.5 %fusion.25 = f32[16,128,128]{2,1,0:T(8,128)S(1)} fusion(s32[16,128,128]{2,1,0:T(8,128)} %copy.63, f32[16,128,128]{2,1,0:T(8,128)} %multiply_reduce_fusion.5, s32[128]{0:T(128)S(1)} %and_select_fusion.2, f32[16,128]{1,0:T(8,128)S(1)} %bitcast.121, f32[16,128]{1,0:T(8,128)S(1)} %bitcast.124, f32[16,128]{1,0:T(8,128)S(1)} %bitcast.122, ...), kind=kLoop, calls=%fused_computation.17.clone.1 | loop fusion | flops 7602176 | bytes 3195392 | tf_op jit(solution)/shard_map/while/body/vmap()/mul | solution.py:46
  60.1 2.1 scatter_fusion.1
  63.4 1.1 copy.51
  64.7 20.4 %collective-permute-start.4 = (f32[3,1,3,4096]{3,2,1,0:T(4,128)S(1)}, f32[3,1,3,4096]{3,2,1,0:T(4,128)S(1)}, u32[]{:S(2)}, u32[]{:S(2)}) collective-permute-start(f32[3,1,3,4096]{3,2,1,0:T(4,128)S(1)} %get-tuple-element.211), channel_id=1, source_target_pairs={{0,8},{8,16},{16,24},{24,0},{1,9},{9,17},{17,25},{25,1},{2,10},{10... | collective-permute-start | bytes 442376 | tf_op jit(solution)/shard_map/ppermute | solution.py:20
  85.8 2.5 %collective-permute-done.4 = f32[3,1,3,4096]{3,2,1,0:T(4,128)S(1)} collective-permute-done((f32[3,1,3,4096]{3,2,1,0:T(4,128)S(1)}, f32[3,1,3,4096]{3,2,1,0:T(4,128)S(1)}, u32[]{:S(2)}, u32[]{:S(2)}) %collective-permute-start.4) | collective-permute-done | bytes 147488 | tf_op jit(solution)/shard_map/ppermute | solution.py:20
  88.5 3.0 %collective-permute-done.5 = f32[3,1,3,4096]{3,2,1,0:T(4,128)S(1)} collective-permute-done((f32[3,1,3,4096]{3,2,1,0:T(4,128)S(1)}, f32[3,1,3,4096]{3,2,1,0:T(4,128)S(1)}, u32[]{:S(2)}, u32[]{:S(2)}) %collective-permute-start.5) | collective-permute-done | bytes 147488 | tf_op jit(solution)/shard_map/ppermute | solution.py:21
  92.1 38.9 %collective-permute-start.6 = (f32[3,5,1,4096]{3,2,1,0:T(1,128)S(1)}, f32[3,5,1,4096]{3,2,1,0:T(1,128)S(1)}, u32[]{:S(2)}, u32[]{:S(2)}) collective-permute-start(f32[3,5,1,4096]{3,2,1,0:T(1,128)S(1)} %get-tuple-element.208), channel_id=1, source_target_pairs={{0,4},{4,0},{1,5},{5,1},{2,6},{6,2},{3,7},{7,3},{8,12},{12,8},{9,1... | collective-permute-start | bytes 737288 | tf_op jit(solution)/shard_map/ppermute | solution.py:20
  131.3 5.0 %copy.53 = f32[3,16384]{0,1:T(8,128)} copy(f32[3,16384]{1,0:T(4,128)S(1)} %bitcast.119) | data formatting | bytes 393216
  137.9 1.7 pad_maximum_fusion.1
  140.8 67.5 %reduce-scatter.4.cloned.1.call-done = f32[4096,3]{1,0:T(8,128)} async-done(((f32[16384,3]{1,0:T(8,128)}), f32[4096,3]{1,0:T(8,128)}) %reduce-scatter.4.cloned.1.call-update) | async-done | bytes 49168
  208.3 2.2 copy.54
  211.9 1.6 collective-permute-start.8
  213.4 2.3 %collective-permute-start.9 = (f32[6,1,3,512]{3,1,2,0:T(1,128)S(1)}, f32[6,1,3,512]{3,1,2,0:T(1,128)S(1)}, u32[]{:S(2)}, u32[]{:S(2)}) collective-permute-start(f32[6,1,3,512]{3,1,2,0:T(1,128)S(1)} %get-tuple-element.215), channel_id=1, source_target_pairs={{8,0},{16,8},{24,16},{0,24},{9,1},{17,9},{25,17},{1,25},{10,2},{18... | collective-permute-start | bytes 110600 | tf_op jit(solution)/shard_map/ppermute | solution.py:21
  215.8 2.4 %collective-permute-done.8 = f32[6,1,3,512]{3,1,2,0:T(1,128)S(1)} collective-permute-done((f32[6,1,3,512]{3,1,2,0:T(1,128)S(1)}, f32[6,1,3,512]{3,1,2,0:T(1,128)S(1)}, u32[]{:S(2)}, u32[]{:S(2)}) %collective-permute-start.8) | collective-permute-done | bytes 36896 | tf_op jit(solution)/shard_map/ppermute | solution.py:20
  218.2 1.5 collective-permute-start.11
  220.3 2.6 %collective-permute-done.11 = f32[6,5,1,512]{3,1,2,0:T(8,128)S(1)} collective-permute-done((f32[6,5,1,512]{3,1,2,0:T(8,128)S(1)}, f32[6,5,1,512]{3,1,2,0:T(8,128)S(1)}, u32[]{:S(2)}, u32[]{:S(2)}) %collective-permute-start.11) | collective-permute-done | bytes 61472 | tf_op jit(solution)/shard_map/ppermute | solution.py:21
  223.0 1.4 collective-permute-done.10
  (90 shorter events, 21.2 us)
Async XLA Ops:
  7.2 37.5 %copy-start.6 = (s32[1,64]{1,0:T(1,128)S(1)}, s32[1,64]{1,0:T(1,128)}, u32[]{:S(2)}) copy-start(s32[1,64]{1,0:T(1,128)} %param.24) | copy-start | bytes 772
  7.2 37.5 %copy-start.5 = (s32[1,64]{1,0:T(1,128)S(1)}, s32[1,64]{1,0:T(1,128)}, u32[]{:S(2)}) copy-start(s32[1,64]{1,0:T(1,128)} %param.25) | copy-start | bytes 772
  7.2 201.1 %reduce-scatter.4.cloned.1.call-start = ((), (), s32[]{:S(2)}) async-start(), calls=%async_computation.1 | async-start | bytes 10485760
  11.9 11.6 %copy-start = (f32[3,4096]{1,0:T(4,128)}, f32[3,4096]{1,0:T(4,128)S(1)}, u32[]{:S(2)}) copy-start(f32[3,4096]{1,0:T(4,128)S(1)} %get-tuple-element.196) | copy-start | bytes 147460
  12.7 9.5 %collective-permute-start = (f32[6,1,1,4096]{3,0,2,1:T(8,128)S(1)}, f32[6,1,1,4096]{3,0,2,1:T(8,128)S(1)}, u32[]{:S(2)}, u32[]{:S(2)}) collective-permute-start(f32[6,1,1,4096]{3,0,2,1:T(8,128)S(1)} %get-tuple-element.216), channel_id=1, source_target_pairs={{0,8},{8,16},{16,24},{24,0},{1,9},{9,17},{17,25},{25,1},{2,10},{10... | collective-permute-start | bytes 294920 | tf_op jit(solution)/shard_map/ppermute | solution.py:20
  15.8 7.8 %collective-permute-start.1 = (f32[6,1,1,4096]{3,0,2,1:T(8,128)S(1)}, f32[6,1,1,4096]{3,0,2,1:T(8,128)S(1)}, u32[]{:S(2)}, u32[]{:S(2)}) collective-permute-start(f32[6,1,1,4096]{3,0,2,1:T(8,128)S(1)} %get-tuple-element.216), channel_id=1, source_target_pairs={{8,0},{16,8},{24,16},{0,24},{9,1},{17,9},{25,17},{1,25},{10,2},{18... | collective-permute-start | bytes 294920 | tf_op jit(solution)/shard_map/ppermute | solution.py:21
  23.6 12.1 %collective-permute-start.2 = (f32[6,3,1,4096]{3,0,2,1:T(8,128)S(1)}, f32[6,3,1,4096]{3,0,2,1:T(8,128)S(1)}, u32[]{:S(2)}, u32[]{:S(2)}) collective-permute-start(f32[6,3,1,4096]{3,0,2,1:T(8,128)S(1)} %pad_maximum_fusion.3), channel_id=1, source_target_pairs={{0,4},{4,0},{1,5},{5,1},{2,6},{6,2},{3,7},{7,3},{8,12},{12,8},{9,1... | collective-permute-start | bytes 884744 | tf_op jit(solution)/shard_map/ppermute | solution.py:20
  25.2 17.4 %collective-permute-start.3 = (f32[6,3,1,4096]{3,0,2,1:T(8,128)S(1)}, f32[6,3,1,4096]{3,0,2,1:T(8,128)S(1)}, u32[]{:S(2)}, u32[]{:S(2)}) collective-permute-start(f32[6,3,1,4096]{3,0,2,1:T(8,128)S(1)} %pad_maximum_fusion.3), channel_id=1, source_target_pairs={{4,0},{0,4},{5,1},{1,5},{6,2},{2,6},{7,3},{3,7},{12,8},{8,12},{13,... | collective-permute-start | bytes 884744 | tf_op jit(solution)/shard_map/ppermute | solution.py:21
  59.1 4.2 %copy-start.7 = (s32[1,64]{1,0:T(1,128)S(1)}, s32[1,64]{1,0:T(1,128)}, u32[]{:S(2)}) copy-start(s32[1,64]{1,0:T(1,128)} %get-tuple-element.403) | copy-start | bytes 772 | tf_op jit(solution)/shard_map/while
  63.4 67.7 %copy-start.8 = (s32[4]{0:T(128)S(1)}, s32[4]{0:T(128)}, u32[]{:S(2)}) copy-start(s32[4]{0:T(128)} %fusion.12) | copy-start | bytes 52
  64.7 23.6 %collective-permute-start.4 = (f32[3,1,3,4096]{3,2,1,0:T(4,128)S(1)}, f32[3,1,3,4096]{3,2,1,0:T(4,128)S(1)}, u32[]{:S(2)}, u32[]{:S(2)}) collective-permute-start(f32[3,1,3,4096]{3,2,1,0:T(4,128)S(1)} %get-tuple-element.211), channel_id=1, source_target_pairs={{0,8},{8,16},{16,24},{24,0},{1,9},{9,17},{17,25},{25,1},{2,10},{10... | collective-permute-start | bytes 442376 | tf_op jit(solution)/shard_map/ppermute | solution.py:20
  85.8 5.7 %collective-permute-start.5 = (f32[3,1,3,4096]{3,2,1,0:T(4,128)S(1)}, f32[3,1,3,4096]{3,2,1,0:T(4,128)S(1)}, u32[]{:S(2)}, u32[]{:S(2)}) collective-permute-start(f32[3,1,3,4096]{3,2,1,0:T(4,128)S(1)} %get-tuple-element.210), channel_id=1, source_target_pairs={{8,0},{16,8},{24,16},{0,24},{9,1},{17,9},{25,17},{1,25},{10,2},{18... | collective-permute-start | bytes 442376 | tf_op jit(solution)/shard_map/ppermute | solution.py:21
  92.1 44.3 %collective-permute-start.6 = (f32[3,5,1,4096]{3,2,1,0:T(1,128)S(1)}, f32[3,5,1,4096]{3,2,1,0:T(1,128)S(1)}, u32[]{:S(2)}, u32[]{:S(2)}) collective-permute-start(f32[3,5,1,4096]{3,2,1,0:T(1,128)S(1)} %get-tuple-element.208), channel_id=1, source_target_pairs={{0,4},{4,0},{1,5},{5,1},{2,6},{6,2},{3,7},{7,3},{8,12},{12,8},{9,1... | collective-permute-start | bytes 737288 | tf_op jit(solution)/shard_map/ppermute | solution.py:20
  131.0 6.9 %collective-permute-start.7 = (f32[3,5,1,4096]{3,2,1,0:T(1,128)S(1)}, f32[3,5,1,4096]{3,2,1,0:T(1,128)}, u32[]{:S(2)}, u32[]{:S(2)}) collective-permute-start(f32[3,5,1,4096]{3,2,1,0:T(1,128)S(1)} %get-tuple-element.209), channel_id=1, source_target_pairs={{4,0},{0,4},{5,1},{1,5},{6,2},{2,6},{7,3},{3,7},{12,8},{8,12},{13,... | collective-permute-start | bytes 737288 | tf_op jit(solution)/shard_map/ppermute | solution.py:21
  136.3 74.2 %copy-start.2 = (f32[3,4096]{1,0:T(4,128)S(1)}, f32[3,4096]{1,0:T(4,128)}, u32[]{:S(2)}) copy-start(f32[3,4096]{1,0:T(4,128)} %param.17) | copy-start | bytes 147460
  136.3 74.1 %copy-start.3 = (f32[3,4096]{1,0:T(4,128)S(1)}, f32[3,4096]{1,0:T(4,128)}, u32[]{:S(2)}) copy-start(f32[3,4096]{1,0:T(4,128)} %param.18) | copy-start | bytes 147460
  136.3 74.9 %copy-start.1 = (f32[3,4096]{1,0:T(4,128)S(1)}, f32[3,4096]{1,0:T(4,128)}, u32[]{:S(2)}) copy-start(f32[3,4096]{1,0:T(4,128)} %copy-done) | copy-start | bytes 147460
  136.4 0.7 copy-start.4
  211.9 6.3 %collective-permute-start.8 = (f32[6,1,3,512]{3,1,2,0:T(1,128)S(1)}, f32[6,1,3,512]{3,1,2,0:T(1,128)S(1)}, u32[]{:S(2)}, u32[]{:S(2)}) collective-permute-start(f32[6,1,3,512]{3,1,2,0:T(1,128)S(1)} %get-tuple-element.214), channel_id=1, source_target_pairs={{0,8},{8,16},{16,24},{24,0},{1,9},{9,17},{17,25},{25,1},{2,10},{10... | collective-permute-start | bytes 110600 | tf_op jit(solution)/shard_map/ppermute | solution.py:20
  213.4 4.7 %collective-permute-start.9 = (f32[6,1,3,512]{3,1,2,0:T(1,128)S(1)}, f32[6,1,3,512]{3,1,2,0:T(1,128)S(1)}, u32[]{:S(2)}, u32[]{:S(2)}) collective-permute-start(f32[6,1,3,512]{3,1,2,0:T(1,128)S(1)} %get-tuple-element.215), channel_id=1, source_target_pairs={{8,0},{16,8},{24,16},{0,24},{9,1},{17,9},{25,17},{1,25},{10,2},{18... | collective-permute-start | bytes 110600 | tf_op jit(solution)/shard_map/ppermute | solution.py:21
  218.2 4.7 %collective-permute-start.11 = (f32[6,5,1,512]{3,1,2,0:T(8,128)S(1)}, f32[6,5,1,512]{3,1,2,0:T(8,128)S(1)}, u32[]{:S(2)}, u32[]{:S(2)}) collective-permute-start(f32[6,5,1,512]{3,1,2,0:T(8,128)S(1)} %get-tuple-element.212), channel_id=1, source_target_pairs={{4,0},{0,4},{5,1},{1,5},{6,2},{2,6},{7,3},{3,7},{12,8},{8,12},{13,... | collective-permute-start | bytes 184328 | tf_op jit(solution)/shard_map/ppermute | solution.py:21
  219.8 4.6 %collective-permute-start.10 = (f32[6,5,1,512]{3,1,2,0:T(8,128)S(1)}, f32[6,5,1,512]{3,1,2,0:T(8,128)S(1)}, u32[]{:S(2)}, u32[]{:S(2)}) collective-permute-start(f32[6,5,1,512]{3,1,2,0:T(8,128)S(1)} %get-tuple-element.213), channel_id=1, source_target_pairs={{0,4},{4,0},{1,5},{5,1},{2,6},{6,2},{3,7},{7,3},{8,12},{12,8},{9,1... | collective-permute-start | bytes 184328 | tf_op jit(solution)/shard_map/ppermute | solution.py:20
Sparse Core Ops, SparseCore 0:
  136.4 71.7 reduce-scatter.3
where the time goes:
time: 234 us; the launch traced here: 232 us
  waiting for transfers between devices  92.7 us (40%)
  starting transfers between devices  72.7 us (31%)
  local copies, waits for them, and re-layouts  22.6 us (10%)
  other arithmetic  20.6 us (9%)
  between operations  14.9 us (6%)
  blocking collectives  7.6 us (3%)
    unnamed x2, waiting for transfers between devices  67.5 us
    ppermute x6, starting transfers between devices, with_halo(): before = lax.ppermute(last, axis, up)  66.1 us
    ppermute x6, waiting for transfers between devices, with_halo(): after = lax.ppermute(first, axis, down)  14.7 us
    ppermute x6, waiting for transfers between devices, with_halo(): before = lax.ppermute(last, axis, up)  10.5 us
    unnamed x22, local copies, waits for them, and re-layouts  8.27 us
    all_gather x1, blocking collectives, local(): lax.all_gather(features, 'gz', axis=1, tiled=True)  7.6 us
    ppermute x6, starting transfers between devices, with_halo(): after = lax.ppermute(first, axis, down)  6.54 us
  transfers between devices with their start and end apart: 13, of which 11 were waited for; matrix products, arithmetic and copies ran while one was open for 5% of the time, Pallas kernels for 0%

commit v1 on v0

v1 whole, which is shorter than its diff:
```python
import functools
import jax
import jax.numpy as jnp
from jax import lax
from jax.experimental import pallas as pl
from jax.experimental.pallas import tpu as pltpu
from jax.sharding import PartitionSpec as P

time_step = 0.2
soft_core = 0.09
cutoff_sq = 1.44
coulomb_k = 0.5
MESH = pl.DeviceIdType.MESH
source_offsets = ((-1, -1), (-1, 0), (-1, 1), (0, -1), (0, 1), (1, -1), (1, 0), (1, 1))
GROUP = 2


class Slots:
    def __init__(self, nx, ny, nz):
        self.nx, self.ny, self.nz = nx, ny, nz
        self.offsets = [(0, 0, 0)] + [(0, 0, k) for k in range(1, nz)]
        self.cell = {(0, 0): 0}
        for da in range(-1, 2):
            for db in range(-1, 2):
                key = (da % nx, db % ny)
                if key not in self.cell:
                    self.cell[key] = len(self.offsets)
                    self.offsets.append((key[0], key[1], 0))
        self.count = len(self.offsets)

    def cell_slot(self, da, db):
        return self.cell[(da % self.nx, db % self.ny)]

    def opposite(self, slot):
        dx, dy, dz = self.offsets[slot]
        if dz:
            return (self.nz - dz) % self.nz
        return self.cell_slot(-dx, -dy)

    def device(self, slot):
        dx, dy, dz = self.offsets[slot]
        return (
            lax.rem(lax.axis_index("gx") + dx, self.nx),
            lax.rem(lax.axis_index("gy") + dy, self.ny),
            lax.rem(lax.axis_index("gz") + dz, self.nz),
        )


def greet(slots):
    barrier = pltpu.get_barrier_semaphore()
    for s in range(1, slots.count):
        pl.semaphore_signal(barrier, inc=1, device_id=slots.device(s), device_id_type=MESH)
    pl.semaphore_wait(barrier, slots.count - 1)


def gather_kernel(
    slots, sigma_ref, eps_ref, pos, vel, fold, mass, charge, species, feats, kinds, send, recv, send2, recv2
):
    blocks = species.shape[1]
    half = vel[...] + 0.5 * time_step * fold[...] * mass[...]
    feats[0, 0:3, :] = pos[...] + time_step * half
    feats[0, 3:4, :] = charge[...]
    which = species[...]
    sigma = jnp.zeros((1, blocks), jnp.float32)
    eps = jnp.zeros((1, blocks), jnp.float32)
    for k in range(sigma_ref.shape[0]):
        sigma = jnp.where(which == k, sigma_ref[k], sigma)
        eps = jnp.where(which == k, eps_ref[k], eps)
    kinds[0] = jnp.zeros(kinds.shape[1:], jnp.float32)
    kinds[0, 0:1, 0:blocks] = sigma
    kinds[0, 1:2, 0:blocks] = jnp.sqrt(eps)
    greet(slots)
    copies = []
    for s in range(1, slots.count):
        there = slots.opposite(s)
        for ref, ss, rs in ((kinds, send2, recv2), (feats, send, recv)):
            copy = pltpu.make_async_remote_copy(
                src_ref=ref.at[0],
                dst_ref=ref.at[there],
                send_sem=ss.at[s],
                recv_sem=rs.at[there],
                device_id=slots.device(s),
                device_id_type=MESH,
            )
            copy.start()
            copies.append(copy)
    for copy in copies:
        copy.wait()


def pair_kernel(slots, blocks, tower, plate, counts, kinds, feats, excl, acc, cell_table):
    width = excl.shape[-1]
    words = excl.shape[2]
    lanes8 = width // words
    nx, ny, nz = slots.nx, slots.ny, slots.nz
    lx, ly = float(nx), float(ny)
    my_layer = lax.axis_index("gz")
    for o in range(9):
        cell_table[o] = slots.cell_slot(o // 3 - 1, o % 3 - 1)
    acc[...] = jnp.zeros(acc.shape, acc.dtype)
    count = counts[0]
    bit = jnp.left_shift(1, lax.broadcasted_iota(jnp.int32, (lanes8, width), 0))
    lane = lax.broadcasted_iota(jnp.int32, (lanes8, width), 1)
    shift_h = soft_core / (lx * lx)
    edge = (cutoff_sq + soft_core) / (lx * lx)
    ratio = (ly / lx) ** 2
    scale = lx * lx / (cutoff_sq * cutoff_sq)

    def one_slot(k, listed):
        t = tower[0, k]
        p = plate[0, k]
        t_slot = lax.rem(t // blocks - my_layer + nz, nz)
        p_slot = cell_table[p // blocks]
        t_block = lax.rem(t, blocks)
        p_block = lax.rem(p, blocks)
        sig = 0.5 * (kinds[t_slot, 0, t_block] + kinds[p_slot, 0, p_block])
        depth = kinds[t_slot, 1, t_block] * kinds[p_slot, 1, p_block]
        sig2 = sig * sig
        sig6 = sig2 * sig2 * sig2
        live = jnp.where(listed, jnp.float32(1.0), jnp.float32(0.0))
        att = (6.0 * scale / lx**6) * depth * sig6 * live
        rep = (12.0 * scale / lx**12) * depth * sig6 * sig6 * live
        t_at = pl.ds(pl.multiple_of(t_block * width, width), width)
        p_at = pl.ds(pl.multiple_of(p_block * width, width), width)
        rows = feats[t_slot, :, t_at]
        prow = feats[p_slot, :, p_at]
        full = (lanes8, width)
        tx = jnp.broadcast_to(rows[0:1] * (1.0 / lx), full)
        ty = jnp.broadcast_to(rows[1:2] * (1.0 / ly), full)
        tz = jnp.broadcast_to(rows[2:3] * (1.0 / lx), full)
        tq = jnp.broadcast_to(rows[3:4] * (coulomb_k * scale / lx) * live, full)
        cols = jnp.concatenate(
            [prow[0:1] * (1.0 / lx), prow[1:2] * (1.0 / ly), prow[2:3] * (1.0 / lx), prow[3:4]] * 2, axis=0
        ).T
        sx = sy = sz = None
        back = []
        for w in range(words):
            piece = cols[w * lanes8 : (w + 1) * lanes8]
            dx = tx - piece[:, 0:1]
            dy = ty - piece[:, 1:2]
            dz = tz - piece[:, 2:3]
            dx = dx - jnp.floor(dx + 0.5)
            dy = dy - jnp.floor(dy + 0.5)
            h = (dx * dx + dz * dz) + (ratio * (dy * dy) + shift_h)
            q = lax.rsqrt(h)
            f = jnp.maximum(edge - h, 0.0)
            s = q * q
            s3 = s * s * s
            g = f * f * s
            e = s3 * (rep * s3 - att) + (tq * piece[:, 3:4]) * q
            c = jnp.where((excl[0, k, w : w + 1, :] & bit) == 0, e * g, 0.0)
            fx, fy, fz = c * dx, c * dy, c * dz
            sx = fx if sx is None else sx + fx
            sy = fy if sy is None else sy + fy
            sz = fz if sz is None else sz + fz
            rx = jnp.sum(fx, axis=1, keepdims=True)
            ry = jnp.sum(fy, axis=1, keepdims=True)
            rz = jnp.sum(fz, axis=1, keepdims=True)
            back.append(jnp.where(lane == 0, rx, jnp.where(lane == 1, ry, rz)))
        on_plate = jnp.concatenate(back, axis=0).T
        lengths = (lx, ly, lx)
        for r, total in enumerate((sx, sy, sz)):
            row = jnp.sum(total, axis=0, keepdims=True) * lengths[r]
            acc[t_slot, r : r + 1, t_at] += row
        for r in range(3):
            acc[p_slot, r : r + 1, p_at] -= on_plate[r : r + 1] * lengths[r]

    def step(i, carry):
        for g in range(GROUP):
            k = i * GROUP + g
            safe = jnp.minimum(k, tower.shape[1] - 1)
            one_slot(safe, k < count)
        return carry

    lax.fori_loop(0, (count + GROUP - 1) // GROUP, step, 0)


def return_kernel(
    slots, blocks, mig_block, mig_dest, acc, pos, vel, fold, mass,
    pos_out, vel_out, force_out, arrive, landed, state, outgoing, arrived, send, recv, send2, recv2,
):
    atoms = pos.shape[1]
    width = atoms // blocks
    leaving = mig_block.shape[1]
    greet(slots)
    copies = []
    for s in range(1, slots.count):
        there = slots.opposite(s)
        copy = pltpu.make_async_remote_copy(
            src_ref=acc.at[s],
            dst_ref=landed.at[there],
            send_sem=send.at[s],
            recv_sem=recv.at[there],
            device_id=slots.device(s),
            device_id_type=MESH,
        )
        copy.start()
        copies.append(copy)
    half = vel[...] + 0.5 * time_step * fold[...] * mass[...]
    moved = pos[...] + time_step * half
    state[0:3, :] = moved
    state[6:8, :] = jnp.zeros((2, atoms), jnp.float32)
    block_of = lax.broadcasted_iota(jnp.int32, (3, atoms), 1) // width
    gone = block_of == mig_block[0, 0]
    for q in range(1, leaving):
        gone = gone | (block_of == mig_block[0, q])
    stay = jnp.where(gone, 0.0, 1.0)
    pos_out[...] = moved * stay
    for copy in copies:
        copy.wait()
    force = acc[0, 0:3, :]
    for s in range(1, slots.count):
        force = force + landed[s, 0:3, :]
    full = half + 0.5 * time_step * force * mass[...]
    state[3:6, :] = full
    for q in range(leaving):
        chosen = jnp.full((8, width), mig_block[0, q], jnp.int32)
        picked = jnp.zeros((8, width), jnp.float32)
        for b in range(blocks):
            picked = jnp.where(chosen == b, state[:, b * width : (b + 1) * width], picked)
        outgoing[0:6, q * width : (q + 1) * width] = picked[0:6]
        outgoing[6:8, q * width : (q + 1) * width] = jnp.full((2, width), mig_dest[0, q], jnp.int32).astype(
            jnp.float32
        )
    force_out[...] = force
    vel_out[...] = full * stay
    near = sorted({slots.cell_slot(a, b) for a, b in source_offsets} - {0})
    copies = []
    for s in near:
        there = slots.opposite(s)
        copy = pltpu.make_async_remote_copy(
            src_ref=outgoing,
            dst_ref=arrived.at[there],
            send_sem=send2.at[s],
            recv_sem=recv2.at[there],
            device_id=slots.device(s),
            device_id_type=MESH,
        )
        copy.start()
        copies.append(copy)
    for copy in copies:
        copy.wait()
    for i, (a, b) in enumerate(source_offsets):
        slot = slots.cell_slot(a, b)
        got = outgoing[...] if slot == 0 else arrived[slot]
        wanted = float((1 - a) * 3 + (1 - b))
        arrive[:, 0, i, :] = jnp.where(got[6:7] == wanted, got[0:6], 0.0)


def local(
    slots, positions, velocities, forces_old, inv_mass, charges, block_species, sigma_table, epsilon_table,
    tower_index, plate_index, tile_counts, exclusions, mig_block, mig_dest,
):
    atoms = positions.shape[1]
    blocks = block_species.shape[0]
    width = atoms // blocks
    n = slots.count
    leaving = mig_block.shape[1]
    vmem = pl.BlockSpec(memory_space=pltpu.VMEM)
    smem = pl.BlockSpec(memory_space=pltpu.SMEM)
    mass = inv_mass[None, :]
    f32 = jnp.float32
    lanes = max(width, blocks)
    sems = pltpu.SemaphoreType.DMA((n,))
    feats, kinds = pl.pallas_call(
        functools.partial(gather_kernel, slots),
        out_shape=(jax.ShapeDtypeStruct((n, 4, atoms), f32), jax.ShapeDtypeStruct((n, 2, lanes), f32)),
        in_specs=[smem, smem] + [vmem] * 6,
        out_specs=(vmem, vmem),
        scratch_shapes=[sems] * 4,
        compiler_params=pltpu.CompilerParams(collective_id=0, has_side_effects=True),
        name="gather_features",
    )(sigma_table, epsilon_table, positions, velocities, forces_old, mass, charges[None, :], block_species[None, :])
    acc = pl.pallas_call(
        functools.partial(pair_kernel, slots, blocks),
        out_shape=jax.ShapeDtypeStruct((n, 4, atoms), f32),
        in_specs=[smem] * 4 + [vmem] * 2,
        out_specs=vmem,
        scratch_shapes=[pltpu.SMEM((9,), jnp.int32)],
        name="pair_forces",
    )(tower_index, plate_index, tile_counts, kinds, feats, exclusions)
    rows = jax.ShapeDtypeStruct((3, atoms), f32)
    return pl.pallas_call(
        functools.partial(return_kernel, slots, blocks),
        out_shape=(rows, rows, rows, jax.ShapeDtypeStruct((6, 1, len(source_offsets), leaving * width), f32)),
        in_specs=[smem] * 2 + [vmem] * 5,
        out_specs=(vmem,) * 4,
        scratch_shapes=[
            pltpu.VMEM((n, 4, atoms), f32),
            pltpu.VMEM((8, atoms), f32),
            pltpu.VMEM((8, leaving * width), f32),
            pltpu.VMEM((n, 8, leaving * width), f32),
        ]
        + [sems] * 4,
        compiler_params=pltpu.CompilerParams(collective_id=1, has_side_effects=True),
        name="return_forces",
    )(mig_block, mig_dest, acc, positions, velocities, forces_old, mass)


def solution(mesh):
    cells = ("gx", "gy", "gz")
    slots = Slots(mesh.shape["gx"], mesh.shape["gy"], mesh.shape["gz"])
    row = P(None, cells)
    flat = P(cells)
    pair = P(cells, None)
    in_specs = (
        row, row, row, flat, flat, flat, P(), P(), pair, pair, flat, P(cells, None, None, None), pair, pair,
    )
    out_specs = (row, row, row, P(None, cells, None, None))
    return jax.shard_map(
        functools.partial(local, slots), mesh=mesh, in_specs=in_specs, out_specs=out_specs, check_vma=False
    )
```

time: 234 us -> 129 us (0.55); the launches traced: 232 us -> 130 us
  Pallas kernels: 0 us -> 125 us
  waiting for transfers between devices: 92.7 us -> 0 us
  starting transfers between devices: 72.7 us -> 0 us
  other arithmetic: 20.6 us -> 0 us
  local copies, waits for them, and re-layouts: 22.6 us -> 3.93 us
  between operations: 14.9 us -> 1.31 us
  blocking collectives: 7.6 us -> 0 us
    pallas_call x0 -> x3, Pallas kernels: none -> 125 us  [the longest x1 89.3 us: local(): pl.pallas_call(functools.partial(return_kernel, slots, blocks), out_shape...]
    ppermute x12 -> x0, starting transfers between devices: 72.7 us -> none  [the longest x6 66.1 us: with_halo(): before = lax.ppermute(last, axis, up)]
    unnamed x2 -> x0, waiting for transfers between devices: 67.5 us -> none
    ppermute x12 -> x0, waiting for transfers between devices: 25.2 us -> none  [the longest x6 14.7 us: with_halo(): after = lax.ppermute(first, axis, down)]
    all_gather x1 -> x0, blocking collectives: 7.6 us -> none  [local(): lax.all_gather(features, 'gz', axis=1, tiled=True)]
    mul x6 -> x0, other arithmetic: 5.65 us -> none  [the longest x1 2.53 us: tile_terms(): (depth_pair * (12.0 * ratio_cube * ratio_cube - 6.0 * ratio_cube) + charg...]
    unnamed x22 -> x10, local copies, waits for them, and re-layouts: 8.27 us -> 3.93 us
    gather x3 -> x0, local copies, waits for them, and re-layouts: 3.98 us -> none  [the longest x1 1.83 us: evaluate(): plate_tiles = jnp.take(plates, plate_ids, axis=1)]
  transfers between devices with their start and end apart: 13 -> 0, of which waited for: 11 -> 0; matrix products, arithmetic and copies ran while one was open for 5% -> 0% of each run, Pallas kernels for 0% -> 0%
where the time goes in v1:
time: 129 us; the launch traced here: 130 us
  Pallas kernels  125 us (97%)
  local copies, waits for them, and re-layouts  3.93 us (3%)
  between operations  1.31 us (1%)
    pallas_call x1, Pallas kernels, local(): pl.pallas_call(functools.partial(return_kernel, slots, blocks), out_shape...  89.3 us
    pallas_call x1, Pallas kernels, local(): pl.pallas_call(functools.partial(pair_kernel, slots, blocks), out_shape=j...  19.8 us
    pallas_call x1, Pallas kernels, local(): pl.pallas_call(functools.partial(gather_kernel, slots), out_shape=(jax.Sh...  15.5 us
    unnamed x10, local copies, waits for them, and re-layouts  3.93 us

profile of v1, /device:TPU:0, one launch (start us, length us, event | category | flops | bytes accessed | tf_op | source)
XLA Modules:
  0.0 129.8 jit_solution(17174369847774948489)
XLA Ops:
  1.3 15.5 %gather_features.1 = (f32[9,4,4096]{2,1,0:T(4,128)}, f32[9,2,128]{2,1,0:T(2,128)}) custom-call(f32[4]{0:T(128)} %sigma_ref.1, f32[4]{0:T(128)} %eps_ref.1, f32[3,4096]{1,0:T(4,128)} %pos.3, f32[3,4096]{1,0:T(4,128)} %vel.3, f32[3,4096]{1,0:T(4,128)} %fold.3, f32[1,4096]{1,0:T(1,128)} %bitcast.3, f32[1,4096]{1,0:T(1,128)} %bitcast.5, s32[1,32]{1,0:T(1,128)} %bitcast.6), custom_call_target="tpu_custom_call" | custom-call | tf_op jit(solution)/shard_map/gather_features/pallas_call | solution.py:265
  16.8 19.8 %pair_forces.1.acc = f32[9,4,4096]{2,1,0:T(4,128)} custom-call(s32[1,64]{1,0:T(1,128)} %tower.1, s32[1,64]{1,0:T(1,128)} %plate.1, s32[1]{0:T(128)S(6)} %copy.22.counts, f32[9,2,128]{2,1,0:T(2,128)} %get-tuple-element.6.kinds, f32[9,4,4096]{2,1,0:T(4,128)} %get-tuple-element.7.feats, s32[1,64,16,128]{3,2,1,0:T(8,128)} %excl.1), custom_call_target="tpu_custom_call" | custom-call | tf_op jit(solution)/shard_map/pair_forces/pallas_call | solution.py:274
  36.6 89.3 %return_forces.1 = (f32[3,4096]{1,0:T(4,128)}, f32[3,4096]{1,0:T(4,128)}, f32[3,4096]{1,0:T(4,128)}, f32[6,1,8,512]{3,2,1,0:T(8,128)}) custom-call(s32[1,4]{1,0:T(1,128)} %mig_block.1, s32[1,4]{1,0:T(1,128)} %mig_dest.1, f32[9,4,4096]{2,1,0:T(4,128)} %pair_forces.1.acc, f32[3,4096]{1,0:T(4,128)} %pos.3, f32[3,4096]{1,0:T(4,128)} %vel.3, f32[3,4096]{1,0:T(4,128)} %fold.3, ...), custom_call_target="tpu_custom_call" | custom-call | tf_op jit(solution)/shard_map/return_forces/pallas_call | solution.py:283
  125.9 0.0 copy-start.2
  125.9 1.5 %copy.23 = f32[3,4096]{1,0:T(4,128)} copy(f32[3,4096]{1,0:T(4,128)} %get-tuple-element.12) | data formatting | bytes 98304
  127.4 0.0 copy-done.2
  127.4 0.0 copy-start.1
  127.4 0.6 copy.24
  128.0 0.2 copy-done.1
  128.2 0.0 copy-start
  128.2 0.6 copy.25
  128.9 0.3 copy-done
  129.2 0.6 copy.26
Async XLA Ops:
  125.9 1.5 %copy-start.2 = (f32[3,4096]{1,0:T(4,128)S(1)}, f32[3,4096]{1,0:T(4,128)}, u32[]{:S(2)}) copy-start(f32[3,4096]{1,0:T(4,128)} %get-tuple-element.13) | copy-start | bytes 147460
  127.4 0.9 copy-start.1
  128.2 0.9 copy-start

commit v2 on v1

--- a/solution.py
+++ b/solution.py
@@ -106,6 +106,21 @@
     ratio = (ly / lx) ** 2
     scale = lx * lx / (cutoff_sq * cutoff_sq)
 
+    sub = lax.broadcasted_iota(jnp.int32, (8, width), 0)
+
+    def three(row):
+        value = jnp.broadcast_to(row, (8, width))
+        high = value.astype(jnp.bfloat16).astype(jnp.float32)
+        rest = value - high
+        mid = rest.astype(jnp.bfloat16).astype(jnp.float32)
+        return [high, mid, rest - mid]
+
+    def by_row(values):
+        made = jnp.zeros((8, width), jnp.float32)
+        for i, v in enumerate(values):
+            made = jnp.where(sub == i, v, made)
+        return made
+
     def one_slot(k, listed):
         t = tower[0, k]
         p = plate[0, k]
@@ -124,21 +139,28 @@
         p_at = pl.ds(pl.multiple_of(p_block * width, width), width)
         rows = feats[t_slot, :, t_at]
         prow = feats[p_slot, :, p_at]
-        full = (lanes8, width)
-        tx = jnp.broadcast_to(rows[0:1] * (1.0 / lx), full)
-        ty = jnp.broadcast_to(rows[1:2] * (1.0 / ly), full)
-        tz = jnp.broadcast_to(rows[2:3] * (1.0 / lx), full)
-        tq = jnp.broadcast_to(rows[3:4] * (coulomb_k * scale / lx) * live, full)
-        cols = jnp.concatenate(
-            [prow[0:1] * (1.0 / lx), prow[1:2] * (1.0 / ly), prow[2:3] * (1.0 / lx), prow[3:4]] * 2, axis=0
-        ).T
+        units = (1.0 / lx, 1.0 / ly, 1.0 / lx)
+        left, right = [], []
+        for r in range(3):
+            left.append(by_row([-v for v in three(prow[r : r + 1] * units[r])] + [1.0, 1.0, 1.0]))
+            right.append(by_row([1.0, 1.0, 1.0] + three(rows[r : r + 1] * units[r])))
+        high, mid, low = three(prow[3:4])
+        left.append(by_row([high, high, high, mid, mid, low]))
+        high, mid, low = three(rows[3:4] * (coulomb_k * scale / lx) * live)
+        right.append(by_row([high, mid, low, high, mid, high]))
+        zero = jnp.zeros((8, width), jnp.float32)
+        left = jnp.concatenate(left, axis=0).T.astype(jnp.bfloat16)
+        right = jnp.concatenate(
+            [jnp.concatenate([right[r] if r == m else zero for r in range(4)], axis=0) for m in range(4)], axis=1
+        ).astype(jnp.bfloat16)
+        made = jnp.dot(left, right, preferred_element_type=jnp.float32)
         sx = sy = sz = None
         back = []
         for w in range(words):
-            piece = cols[w * lanes8 : (w + 1) * lanes8]
-            dx = tx - piece[:, 0:1]
-            dy = ty - piece[:, 1:2]
-            dz = tz - piece[:, 2:3]
+            piece = made[w * lanes8 : (w + 1) * lanes8]
+            dx = piece[:, 0:width]
+            dy = piece[:, width : 2 * width]
+            dz = piece[:, 2 * width : 3 * width]
             dx = dx - jnp.floor(dx + 0.5)
             dy = dy - jnp.floor(dy + 0.5)
             h = (dx * dx + dz * dz) + (ratio * (dy * dy) + shift_h)
@@ -147,7 +169,7 @@
             s = q * q
             s3 = s * s * s
             g = f * f * s
-            e = s3 * (rep * s3 - att) + (tq * piece[:, 3:4]) * q
+            e = s3 * (rep * s3 - att) + piece[:, 3 * width :] * q
             c = jnp.where((excl[0, k, w : w + 1, :] & bit) == 0, e * g, 0.0)
             fx, fy, fz = c * dx, c * dy, c * dz
             sx = fx if sx is None else sx + fx

time: 129 us -> 51.3 us (0.40)
  Pallas kernels: 125 us -> 46 us
    pallas_call x1, Pallas kernels: 89.3 us -> 21.7 us  [local(): pl.pallas_call(functools.partial(return_kernel, slots, blocks), out_shape...]
    pallas_call x1, Pallas kernels: 19.8 us -> 8.89 us  [local(): pl.pallas_call(functools.partial(pair_kernel, slots, blocks), out_shape=j...]
where the time goes in v2:
time: 51.3 us
  Pallas kernels  46 us (90%)
  local copies, waits for them, and re-layouts  3.93 us (8%)
  between operations  1.31 us (3%)
    pallas_call x1, Pallas kernels, local(): pl.pallas_call(functools.partial(return_kernel, slots, blocks), out_shape...  21.7 us
    pallas_call x1, Pallas kernels, local(): pl.pallas_call(functools.partial(gather_kernel, slots), out_shape=(jax.Sh...  15.5 us
    pallas_call x1, Pallas kernels, local(): pl.pallas_call(functools.partial(pair_kernel, slots, blocks), out_shape=j...  8.89 us
    unnamed x10, local copies, waits for them, and re-layouts  3.93 us

profile of v2, /device:TPU:0, one launch (start us, length us, event | category | flops | bytes accessed | tf_op | source)
XLA Modules:
  0.0 51.3 jit_solution(4655209959170995375)
XLA Ops:
  1.3 15.5 %gather_features.1 = (f32[9,4,4096]{2,1,0:T(4,128)}, f32[9,2,128]{2,1,0:T(2,128)}) custom-call(f32[4]{0:T(128)} %sigma_ref.1, f32[4]{0:T(128)} %eps_ref.1, f32[3,4096]{1,0:T(4,128)} %pos.3, f32[3,4096]{1,0:T(4,128)} %vel.3, f32[3,4096]{1,0:T(4,128)} %fold.3, f32[1,4096]{1,0:T(1,128)} %bitcast.3, f32[1,4096]{1,0:T(1,128)} %bitcast.5, s32[1,32]{1,0:T(1,128)} %bitcast.6), custom_call_target="tpu_custom_call" | custom-call | tf_op jit(solution)/shard_map/gather_features/pallas_call | solution.py:287
  16.8 8.9 %pair_forces.1.acc = f32[9,4,4096]{2,1,0:T(4,128)} custom-call(s32[1,64]{1,0:T(1,128)} %tower.1, s32[1,64]{1,0:T(1,128)} %plate.1, s32[1]{0:T(128)S(6)} %copy.22.counts, f32[9,2,128]{2,1,0:T(2,128)} %get-tuple-element.6.kinds, f32[9,4,4096]{2,1,0:T(4,128)} %get-tuple-element.7.feats, s32[1,64,16,128]{3,2,1,0:T(8,128)} %excl.1), custom_call_target="tpu_custom_call" | custom-call | tf_op jit(solution)/shard_map/pair_forces/pallas_call | solution.py:296
  25.7 21.7 %return_forces.1 = (f32[3,4096]{1,0:T(4,128)}, f32[3,4096]{1,0:T(4,128)}, f32[3,4096]{1,0:T(4,128)}, f32[6,1,8,512]{3,2,1,0:T(8,128)}) custom-call(s32[1,4]{1,0:T(1,128)} %mig_block.1, s32[1,4]{1,0:T(1,128)} %mig_dest.1, f32[9,4,4096]{2,1,0:T(4,128)} %pair_forces.1.acc, f32[3,4096]{1,0:T(4,128)} %pos.3, f32[3,4096]{1,0:T(4,128)} %vel.3, f32[3,4096]{1,0:T(4,128)} %fold.3, ...), custom_call_target="tpu_custom_call" | custom-call | tf_op jit(solution)/shard_map/return_forces/pallas_call | solution.py:305
  47.3 0.0 copy-start.2
  47.3 1.5 %copy.23 = f32[3,4096]{1,0:T(4,128)} copy(f32[3,4096]{1,0:T(4,128)} %get-tuple-element.12) | data formatting | bytes 98304
  48.9 0.0 copy-done.2
  48.9 0.0 copy-start.1
  48.9 0.6 %copy.24 = f32[3,4096]{1,0:T(4,128)} copy(f32[3,4096]{1,0:T(4,128)S(1)} %copy-done.2) | data formatting | bytes 98304
  49.5 0.2 copy-done.1
  49.7 0.0 copy-start
  49.7 0.6 %copy.25 = f32[3,4096]{1,0:T(4,128)} copy(f32[3,4096]{1,0:T(4,128)S(1)} %copy-done.1) | data formatting | bytes 98304
  50.4 0.3 copy-done
  50.6 0.6 %copy.26 = f32[6,1,8,512]{3,2,1,0:T(8,128)} copy(f32[6,1,8,512]{3,2,1,0:T(8,128)S(1)} %copy-done) | data formatting | bytes 196608
Async XLA Ops:
  47.3 1.5 %copy-start.2 = (f32[3,4096]{1,0:T(4,128)S(1)}, f32[3,4096]{1,0:T(4,128)}, u32[]{:S(2)}) copy-start(f32[3,4096]{1,0:T(4,128)} %get-tuple-element.13) | copy-start | bytes 147460
  48.9 0.9 %copy-start.1 = (f32[3,4096]{1,0:T(4,128)S(1)}, f32[3,4096]{1,0:T(4,128)}, u32[]{:S(2)}) copy-start(f32[3,4096]{1,0:T(4,128)} %get-tuple-element.14) | copy-start | bytes 147460
  49.7 0.9 %copy-start = (f32[6,1,8,512]{3,2,1,0:T(8,128)S(1)}, f32[6,1,8,512]{3,2,1,0:T(8,128)}, u32[]{:S(2)}) copy-start(f32[6,1,8,512]{3,2,1,0:T(8,128)} %get-tuple-element.15) | copy-start | bytes 294916

commit v3 on v2

--- a/solution.py
+++ b/solution.py
@@ -12,7 +12,6 @@
 coulomb_k = 0.5
 MESH = pl.DeviceIdType.MESH
 source_offsets = ((-1, -1), (-1, 0), (-1, 1), (0, -1), (0, 1), (1, -1), (1, 0), (1, 1))
-GROUP = 2
 
 
 class Slots:
@@ -88,25 +87,39 @@
         copy.wait()
 
 
-def pair_kernel(slots, blocks, tower, plate, counts, kinds, feats, excl, acc, cell_table):
+def stay_rows(mig_block, shape, width):
+    block_of = lax.broadcasted_iota(jnp.int32, shape, 1) // width
+    gone = block_of == mig_block[0, 0]
+    for q in range(1, mig_block.shape[1]):
+        gone = gone | (block_of == mig_block[0, q])
+    return jnp.where(gone, 0.0, 1.0)
+
+
+def pair_kernel(
+    slots, blocks, tower, plate, counts, kinds, mig_block, feats, excl, acc, pos_out, cell_table,
+    made_a, made_b, tail_a, tail_b,
+):
     width = excl.shape[-1]
     words = excl.shape[2]
     lanes8 = width // words
+    last = tower.shape[1] - 1
     nx, ny, nz = slots.nx, slots.ny, slots.nz
     lx, ly = float(nx), float(ny)
     my_layer = lax.axis_index("gz")
     for o in range(9):
         cell_table[o] = slots.cell_slot(o // 3 - 1, o % 3 - 1)
     acc[...] = jnp.zeros(acc.shape, acc.dtype)
+    pos_out[...] = feats[0, 0:3, :] * stay_rows(mig_block, pos_out.shape, width)
     count = counts[0]
     bit = jnp.left_shift(1, lax.broadcasted_iota(jnp.int32, (lanes8, width), 0))
     lane = lax.broadcasted_iota(jnp.int32, (lanes8, width), 1)
+    sub = lax.broadcasted_iota(jnp.int32, (8, width), 0)
     shift_h = soft_core / (lx * lx)
     edge = (cutoff_sq + soft_core) / (lx * lx)
     ratio = (ly / lx) ** 2
     scale = lx * lx / (cutoff_sq * cutoff_sq)
-
-    sub = lax.broadcasted_iota(jnp.int32, (8, width), 0)
+    units = (1.0 / lx, 1.0 / ly, 1.0 / lx)
+    lengths = (lx, ly, lx)
 
     def three(row):
         value = jnp.broadcast_to(row, (8, width))
@@ -121,25 +134,21 @@
             made = jnp.where(sub == i, v, made)
         return made
 
-    def one_slot(k, listed):
+    def place(k):
+        k = jnp.clip(k, 0, last)
         t = tower[0, k]
         p = plate[0, k]
-        t_slot = lax.rem(t // blocks - my_layer + nz, nz)
-        p_slot = cell_table[p // blocks]
-        t_block = lax.rem(t, blocks)
-        p_block = lax.rem(p, blocks)
-        sig = 0.5 * (kinds[t_slot, 0, t_block] + kinds[p_slot, 0, p_block])
-        depth = kinds[t_slot, 1, t_block] * kinds[p_slot, 1, p_block]
-        sig2 = sig * sig
-        sig6 = sig2 * sig2 * sig2
-        live = jnp.where(listed, jnp.float32(1.0), jnp.float32(0.0))
-        att = (6.0 * scale / lx**6) * depth * sig6 * live
-        rep = (12.0 * scale / lx**12) * depth * sig6 * sig6 * live
-        t_at = pl.ds(pl.multiple_of(t_block * width, width), width)
-        p_at = pl.ds(pl.multiple_of(p_block * width, width), width)
-        rows = feats[t_slot, :, t_at]
-        prow = feats[p_slot, :, p_at]
-        units = (1.0 / lx, 1.0 / ly, 1.0 / lx)
+        t_layer = lax.div(t, blocks)
+        t_slot = t_layer - my_layer
+        t_slot = jnp.where(t_slot < 0, t_slot + nz, t_slot)
+        p_cell = lax.div(p, blocks)
+        return t_slot, t - t_layer * blocks, cell_table[p_cell], p - p_cell * blocks
+
+    def prepare(k, made):
+        t_slot, t_block, p_slot, p_block = place(k)
+        live = jnp.where(k < count, jnp.float32(1.0), jnp.float32(0.0))
+        rows = feats[t_slot, :, pl.ds(pl.multiple_of(t_block * width, width), width)]
+        prow = feats[p_slot, :, pl.ds(pl.multiple_of(p_block * width, width), width)]
         left, right = [], []
         for r in range(3):
             left.append(by_row([-v for v in three(prow[r : r + 1] * units[r])] + [1.0, 1.0, 1.0]))
@@ -153,14 +162,24 @@
         right = jnp.concatenate(
             [jnp.concatenate([right[r] if r == m else zero for r in range(4)], axis=0) for m in range(4)], axis=1
         ).astype(jnp.bfloat16)
-        made = jnp.dot(left, right, preferred_element_type=jnp.float32)
-        sx = sy = sz = None
-        back = []
+        made[...] = jnp.dot(left, right, preferred_element_type=jnp.float32)
+
+    def arithmetic(k, made, tail):
+        t_slot, t_block, p_slot, p_block = place(k)
+        safe = jnp.minimum(k, last)
+        sig = 0.5 * (kinds[t_slot, 0, t_block] + kinds[p_slot, 0, p_block])
+        depth = kinds[t_slot, 1, t_block] * kinds[p_slot, 1, p_block]
+        sig2 = sig * sig
+        sig6 = sig2 * sig2 * sig2
+        live = jnp.where(k < count, jnp.float32(1.0), jnp.float32(0.0))
+        att = (6.0 * scale / lx**6) * depth * sig6 * live
+        rep = (12.0 * scale / lx**12) * depth * sig6 * sig6 * live
+        sums = [None, None, None]
         for w in range(words):
-            piece = made[w * lanes8 : (w + 1) * lanes8]
-            dx = piece[:, 0:width]
-            dy = piece[:, width : 2 * width]
-            dz = piece[:, 2 * width : 3 * width]
+            at = slice(w * lanes8, (w + 1) * lanes8)
+            dx = made[at, 0:width]
+            dy = made[at, width : 2 * width]
+            dz = made[at, 2 * width : 3 * width]
             dx = dx - jnp.floor(dx + 0.5)
             dy = dy - jnp.floor(dy + 0.5)
             h = (dx * dx + dz * dz) + (ratio * (dy * dy) + shift_h)
@@ -169,37 +188,45 @@
             s = q * q
             s3 = s * s * s
             g = f * f * s
-            e = s3 * (rep * s3 - att) + piece[:, 3 * width :] * q
-            c = jnp.where((excl[0, k, w : w + 1, :] & bit) == 0, e * g, 0.0)
-            fx, fy, fz = c * dx, c * dy, c * dz
-            sx = fx if sx is None else sx + fx
-            sy = fy if sy is None else sy + fy
-            sz = fz if sz is None else sz + fz
-            rx = jnp.sum(fx, axis=1, keepdims=True)
-            ry = jnp.sum(fy, axis=1, keepdims=True)
-            rz = jnp.sum(fz, axis=1, keepdims=True)
-            back.append(jnp.where(lane == 0, rx, jnp.where(lane == 1, ry, rz)))
-        on_plate = jnp.concatenate(back, axis=0).T
-        lengths = (lx, ly, lx)
-        for r, total in enumerate((sx, sy, sz)):
-            row = jnp.sum(total, axis=0, keepdims=True) * lengths[r]
-            acc[t_slot, r : r + 1, t_at] += row
+            e = s3 * (rep * s3 - att) + made[at, 3 * width : 4 * width] * q
+            c = jnp.where((excl[0, safe, w : w + 1, :] & bit) == 0, e * g, 0.0)
+            parts = (c * dx, c * dy, c * dz)
+            sums = [v if u is None else u + v for u, v in zip(sums, parts)]
+            rx, ry, rz = [jnp.sum(v, axis=1, keepdims=True) for v in parts]
+            tail[at, :] = jnp.where(lane == 0, rx, jnp.where(lane == 1, ry, rz))
+        rows = [acc[t_slot, pl.ds(r * blocks + t_block, 1), :] for r in range(3)]
         for r in range(3):
-            acc[p_slot, r : r + 1, p_at] -= on_plate[r : r + 1] * lengths[r]
+            total = jnp.sum(sums[r], axis=0, keepdims=True) * lengths[r]
+            acc[t_slot, pl.ds(r * blocks + t_block, 1), :] = rows[r] + total
+
+    def finish(k, tail):
+        t_slot, t_block, p_slot, p_block = place(k)
+        on_plate = tail[...].T
+        rows = [acc[p_slot, pl.ds(r * blocks + p_block, 1), :] for r in range(3)]
+        for r in range(3):
+            acc[p_slot, pl.ds(r * blocks + p_block, 1), :] = rows[r] - on_plate[r : r + 1] * lengths[r]
+
+    tail_b[...] = jnp.zeros(tail_b.shape, jnp.float32)
+    prepare(0, made_a)
 
     def step(i, carry):
-        for g in range(GROUP):
-            k = i * GROUP + g
-            safe = jnp.minimum(k, tower.shape[1] - 1)
-            one_slot(safe, k < count)
+        k = i * 2
+        finish(k - 1, tail_b)
+        prepare(k + 1, made_b)
+        arithmetic(k, made_a, tail_a)
+        finish(k, tail_a)
+        prepare(k + 2, made_a)
+        arithmetic(k + 1, made_b, tail_b)
         return carry
 
-    lax.fori_loop(0, (count + GROUP - 1) // GROUP, step, 0)
+    steps = (count + 1) // 2
+    lax.fori_loop(0, steps, step, 0)
+    finish(2 * steps - 1, tail_b)
 
 
 def return_kernel(
     slots, blocks, mig_block, mig_dest, acc, pos, vel, fold, mass,
-    pos_out, vel_out, force_out, arrive, landed, state, outgoing, arrived, send, recv, send2, recv2,
+    vel_full, force_out, arrived, landed, state, outgoing, send, recv, send2, recv2,
 ):
     atoms = pos.shape[1]
     width = atoms // blocks
@@ -219,21 +246,17 @@
         copy.start()
         copies.append(copy)
     half = vel[...] + 0.5 * time_step * fold[...] * mass[...]
-    moved = pos[...] + time_step * half
-    state[0:3, :] = moved
+    state[0:3, :] = pos[...] + time_step * half
     state[6:8, :] = jnp.zeros((2, atoms), jnp.float32)
-    block_of = lax.broadcasted_iota(jnp.int32, (3, atoms), 1) // width
-    gone = block_of == mig_block[0, 0]
-    for q in range(1, leaving):
-        gone = gone | (block_of == mig_block[0, q])
-    stay = jnp.where(gone, 0.0, 1.0)
-    pos_out[...] = moved * stay
     for copy in copies:
         copy.wait()
-    force = acc[0, 0:3, :]
+    force = acc[0]
     for s in range(1, slots.count):
-        force = force + landed[s, 0:3, :]
-    full = half + 0.5 * time_step * force * mass[...]
+        force = force + landed[s]
+    for r in range(3):
+        for b in range(blocks):
+            force_out[r : r + 1, b * width : (b + 1) * width] = force[r * blocks + b : r * blocks + b + 1]
+    full = half + 0.5 * time_step * force_out[...] * mass[...]
     state[3:6, :] = full
     for q in range(leaving):
         chosen = jnp.full((8, width), mig_block[0, q], jnp.int32)
@@ -244,9 +267,11 @@
         outgoing[6:8, q * width : (q + 1) * width] = jnp.full((2, width), mig_dest[0, q], jnp.int32).astype(
             jnp.float32
         )
-    force_out[...] = force
-    vel_out[...] = full * stay
+    vel_full[...] = full
+    arrived[0] = outgoing[...]
     near = sorted({slots.cell_slot(a, b) for a, b in source_offsets} - {0})
+    for s in range(1, slots.nz):
+        arrived[s] = jnp.zeros(arrived.shape[1:], jnp.float32)
     copies = []
     for s in near:
         there = slots.opposite(s)
@@ -262,9 +287,14 @@
         copies.append(copy)
     for copy in copies:
         copy.wait()
+
+
+def output_kernel(slots, blocks, mig_block, force, full, arrived, force_out, vel_out, arrive):
+    width = force.shape[1] // blocks
+    force_out[...] = force[...]
+    vel_out[...] = full[...] * stay_rows(mig_block, full.shape, width)
     for i, (a, b) in enumerate(source_offsets):
-        slot = slots.cell_slot(a, b)
-        got = outgoing[...] if slot == 0 else arrived[slot]
+        got = arrived[slots.cell_slot(a, b)]
         wanted = float((1 - a) * 3 + (1 - b))
         arrive[:, 0, i, :] = jnp.where(got[6:7] == wanted, got[0:6], 0.0)
 
@@ -293,30 +323,41 @@
         compiler_params=pltpu.CompilerParams(collective_id=0, has_side_effects=True),
         name="gather_features",
     )(sigma_table, epsilon_table, positions, velocities, forces_old, mass, charges[None, :], block_species[None, :])
-    acc = pl.pallas_call(
+    rows = jax.ShapeDtypeStruct((3, atoms), f32)
+    packed = jax.ShapeDtypeStruct((n, 3 * blocks, width), f32)
+    acc, positions_new = pl.pallas_call(
         functools.partial(pair_kernel, slots, blocks),
-        out_shape=jax.ShapeDtypeStruct((n, 4, atoms), f32),
-        in_specs=[smem] * 4 + [vmem] * 2,
-        out_specs=vmem,
-        scratch_shapes=[pltpu.SMEM((9,), jnp.int32)],
+        out_shape=(packed, rows),
+        in_specs=[smem] * 5 + [vmem] * 2,
+        out_specs=(vmem, vmem),
+        scratch_shapes=[pltpu.SMEM((9,), jnp.int32)]
+        + [pltpu.VMEM((width, 4 * width), f32)] * 2
+        + [pltpu.VMEM((width, width), f32)] * 2,
         name="pair_forces",
-    )(tower_index, plate_index, tile_counts, kinds, feats, exclusions)
-    rows = jax.ShapeDtypeStruct((3, atoms), f32)
-    return pl.pallas_call(
+    )(tower_index, plate_index, tile_counts, kinds, mig_block, feats, exclusions)
+    strip = jax.ShapeDtypeStruct((n, 8, leaving * width), f32)
+    full, force, arrived = pl.pallas_call(
         functools.partial(return_kernel, slots, blocks),
-        out_shape=(rows, rows, rows, jax.ShapeDtypeStruct((6, 1, len(source_offsets), leaving * width), f32)),
+        out_shape=(rows, rows, strip),
         in_specs=[smem] * 2 + [vmem] * 5,
-        out_specs=(vmem,) * 4,
+        out_specs=(vmem,) * 3,
         scratch_shapes=[
-            pltpu.VMEM((n, 4, atoms), f32),
+            pltpu.VMEM(packed.shape, f32),
             pltpu.VMEM((8, atoms), f32),
             pltpu.VMEM((8, leaving * width), f32),
-            pltpu.VMEM((n, 8, leaving * width), f32),
         ]
         + [sems] * 4,
         compiler_params=pltpu.CompilerParams(collective_id=1, has_side_effects=True),
         name="return_forces",
     )(mig_block, mig_dest, acc, positions, velocities, forces_old, mass)
+    forces_new, velocities_new, arrivals = pl.pallas_call(
+        functools.partial(output_kernel, slots, blocks),
+        out_shape=(rows, rows, jax.ShapeDtypeStruct((6, 1, len(source_offsets), leaving * width), f32)),
+        in_specs=[smem] + [vmem] * 3,
+        out_specs=(vmem,) * 3,
+        name="outputs",
+    )(mig_block, force, full, arrived)
+    return positions_new, velocities_new, forces_new, arrivals
 
 
 def solution(mesh):

time: 51.3 us -> 48.6 us (0.947)
  local copies, waits for them, and re-layouts: 3.93 us -> 0 us
  Pallas kernels: 46 us -> 47.6 us
    pallas_call x1 -> x2, Pallas kernels: 8.89 us -> 18.7 us  [the longest x1 16.9 us: local(): pl.pallas_call(functools.partial(pair_kernel, slots, blocks), out_shape=(...]
    pallas_call x1, Pallas kernels: 21.7 us -> 13.4 us  [local(): pl.pallas_call(functools.partial(return_kernel, slots, blocks), out_shape...]
    unnamed x10 -> x0, local copies, waits for them, and re-layouts: 3.93 us -> none
where the time goes in v3:
time: 48.6 us; the launch traced here: 48.9 us
  Pallas kernels  47.6 us (98%)
  between operations  1.3 us (3%)
    pallas_call x1, Pallas kernels, local(): pl.pallas_call(functools.partial(pair_kernel, slots, blocks), out_shape=(...  16.9 us
    pallas_call x1, Pallas kernels, local(): pl.pallas_call(functools.partial(gather_kernel, slots), out_shape=(jax.Sh...  15.5 us
    pallas_call x1, Pallas kernels, local(): pl.pallas_call(functools.partial(return_kernel, slots, blocks), out_shape...  13.4 us
    pallas_call x1, Pallas kernels, local(): pl.pallas_call(functools.partial(output_kernel, slots, blocks), out_shape...  1.72 us

profile of v3, /device:TPU:0, one launch (start us, length us, event | category | flops | bytes accessed | tf_op | source)
XLA Modules:
  0.0 48.9 jit_solution(13632716177252806272)
XLA Ops:
  1.3 15.5 %gather_features.1 = (f32[9,4,4096]{2,1,0:T(4,128)}, f32[9,2,128]{2,1,0:T(2,128)}) custom-call(f32[4]{0:T(128)} %sigma_ref.1, f32[4]{0:T(128)} %eps_ref.1, f32[3,4096]{1,0:T(4,128)} %pos.3, f32[3,4096]{1,0:T(4,128)} %vel.3, f32[3,4096]{1,0:T(4,128)} %fold.3, f32[1,4096]{1,0:T(1,128)} %bitcast.3, f32[1,4096]{1,0:T(1,128)} %bitcast.5, s32[1,32]{1,0:T(1,128)} %bitcast.6), custom_call_target="tpu_custom_call" | custom-call | tf_op jit(solution)/shard_map/gather_features/pallas_call | solution.py:317
  16.8 16.9 %pair_forces.1 = (f32[9,96,128]{2,1,0:T(8,128)}, f32[3,4096]{1,0:T(4,128)}) custom-call(s32[1,64]{1,0:T(1,128)} %tower.1, s32[1,64]{1,0:T(1,128)} %plate.1, s32[1]{0:T(128)S(6)} %copy.18.counts, f32[9,2,128]{2,1,0:T(2,128)} %get-tuple-element.14.kinds, s32[1,4]{1,0:T(1,128)} %mig_block.5, f32[9,4,4096]{2,1,0:T(4,128)} %get-tuple-element.15.feats, ...), custom_call_target="tpu_custom_call" | custom-call | tf_op jit(solution)/shard_map/pair_forces/pallas_call | solution.py:328
  33.7 13.4 %return_forces.1 = (f32[3,4096]{1,0:T(4,128)}, f32[3,4096]{1,0:T(4,128)}, f32[9,8,512]{2,1,0:T(8,128)}) custom-call(s32[1,4]{1,0:T(1,128)} %mig_block.5, s32[1,4]{1,0:T(1,128)} %mig_dest.1, f32[9,96,128]{2,1,0:T(8,128)} %get-tuple-element.17.acc, f32[3,4096]{1,0:T(4,128)} %pos.3, f32[3,4096]{1,0:T(4,128)} %vel.3, f32[3,4096]{1,0:T(4,128)} %fold.3, ...), custom_call_target="tpu_custom_call" | custom-call | tf_op jit(solution)/shard_map/return_forces/pallas_call | solution.py:339
  47.2 1.7 %outputs.1 = (f32[3,4096]{1,0:T(4,128)}, f32[3,4096]{1,0:T(4,128)}, f32[6,1,8,512]{3,2,1,0:T(8,128)}) custom-call(s32[1,4]{1,0:T(1,128)} %mig_block.5, f32[3,4096]{1,0:T(4,128)} %get-tuple-element.18.force, f32[3,4096]{1,0:T(4,128)} %get-tuple-element.19.full, f32[9,8,512]{2,1,0:T(8,128)} %get-tuple-element.20.arrived), custom_call_target="tpu_custom_call" | custom-call | tf_op jit(solution)/shard_map/outputs/pallas_call | solution.py:353
